TPU v7x, 32 devices: a whole 2x2x4 slice. The times are simulated.
32 devices in a mesh: region: 4 (over y, x), cluster: 8 (over z, core).
Axes of the slice: x: 2, y: 2, z: 4, core: 2. Of those that a mesh axis runs over, the one named last changes fastest.
Arguments:
- pilots: bfloat16 [128, 1024, 1024], P(('region', 'cluster')), may hold values from -0.1875 to 0.1875
- estimate: bfloat16 [128, 8, 1024], P(('region', 'cluster')), may hold values from -6 to 6
- visible: int32 [128, 1024], P(('region', 'cluster')), may hold values from 0 to 65535, as said below
- blocks: int32 [128], P(('region', 'cluster')), may hold values from 4 to 8
- received: float32 [128, 8, 1024], P(('region', 'cluster')), may hold values from -6 to 6
- previous: float32 [128, 8, 1024], P(('region', 'cluster')), may hold values from -6 to 6
- onsager: float32 [128], P(('region', 'cluster')), may hold values from 0.2 to 0.8
- user_cluster: int32 [65536], replicated, may hold values from 0 to 15
- cluster_prior: float32 [16], replicated, may hold values from -4 to 0
Outputs:
- new_estimate: bfloat16 [128, 8, 1024], P(('region', 'cluster'))
- residual: float32 [128, 8, 1024], P(('region', 'cluster'))
- posterior: float32 [65536], P(('region', 'cluster'))
Inputs may be any that keep to these rules, and one draw needn't show every extreme that they name: Every draw has some access point with 8 live blocks. `visible`: users are numbered region by region, 2048 * 8 to a region, in the order of the devices along region+cluster. An access point hears only users of its own region or of the two regions beside it along region (the first and the last region are beside each other); most of the users it hears are of its own region.
All inputs are finite; a program needn't handle non-finite values.
Results may differ from a plain program's by a relative error of at most 0.0056.
Values sent between devices are 32-bit elements; how exact they have to be, the bound alone decides.
A program may use at most 192 MiB of HBM per device.

v0:
```python
import jax
import jax.numpy as jnp
from jax import lax
from jax.sharding import PartitionSpec as P

ROW_BLOCK = 128
U_DEV = 2048
epsilon = 1e-06


def passed_along(block, axis, distance):
    devices = range(lax.axis_size(axis))
    route = [((i - distance) % len(devices), i) for i in devices]
    return lax.ppermute(block, axis, route)


def decide(summed, start, count, user_cluster, cluster_prior):
    labels = lax.dynamic_slice_in_dim(user_cluster, start, count)
    table = jnp.arange(cluster_prior.shape[0], dtype=jnp.int32)
    prior = jnp.sum(
        jnp.where(labels[:, None] == table[None, :], cluster_prior[None, :], jnp.float32(0.0)),
        axis=1,
    )
    return jax.nn.sigmoid(summed + prior)


def local(
    pilots, estimate, visible, blocks, received, previous, onsager, user_cluster, cluster_prior
):
    points, antennas, slots = estimate.shape
    live = jnp.arange(slots)[None, :] // ROW_BLOCK < blocks[:, None]
    masked = jnp.where(live[:, None, :], estimate, jnp.zeros_like(estimate))
    widened = masked.astype(jnp.float32)
    product = jnp.einsum("amr,arl->aml", masked, pilots, preferred_element_type=jnp.float32)
    resid = received - product + onsager[:, None, None] * previous
    spread = jnp.mean(resid * resid, axis=(1, 2)) + epsilon
    narrow = resid.astype(jnp.bfloat16)
    stat = widened + jnp.einsum("aml,arl->amr", narrow, pilots, preferred_element_type=jnp.float32)
    energy = jnp.sum(stat * stat, axis=1)
    base = 0.5 * antennas * jnp.log(spread / (1.0 + spread))
    llr = base[:, None] + energy / (2.0 * spread * (1.0 + spread))[:, None]
    llr = jnp.where(live, llr, jnp.float32(0.0))
    total_users = U_DEV * lax.axis_size("region") * lax.axis_size("cluster")
    own_start = lax.axis_index(("region", "cluster")) * U_DEV
    flat_llr = llr.reshape(-1)
    region_users = U_DEV * lax.axis_size("cluster")
    regions = lax.axis_size("region")
    lowest = (lax.axis_index("region") + regions - 1) % regions * region_users
    relative = (visible - lowest + total_users) % total_users
    window = jax.ops.segment_sum(flat_llr, relative.reshape(-1), num_segments=3 * region_users)
    from_below = passed_along(window[2 * region_users :], "region", 1)
    from_above = passed_along(window[:region_users], "region", -1)
    region_sum = window[region_users : 2 * region_users] + from_below + from_above
    owned_sum = lax.psum_scatter(region_sum, "cluster", scatter_dimension=0, tiled=True)
    owned = decide(owned_sum, own_start, U_DEV, user_cluster, cluster_prior)
    own_post = lax.all_gather(owned, "cluster", axis=0, tiled=True)
    below = passed_along(own_post, "region", 1)
    above = passed_along(own_post, "region", -1)
    nearby = jnp.concatenate([below, own_post, above])
    rate = nearby[relative]
    fresh = rate[:, None, :] * stat / (1.0 + spread)[:, None, None]
    new_estimate = jnp.where(live[:, None, :], fresh, jnp.float32(0.0)).astype(jnp.bfloat16)
    return (new_estimate, resid, owned)


def solution(mesh):
    placed = (
        P(("region", "cluster"), None, None),
        P(("region", "cluster"), None, None),
        P(("region", "cluster"), None),
        P(("region", "cluster")),
        P(("region", "cluster"), None, None),
        P(("region", "cluster"), None, None),
        P(("region", "cluster")),
        P(),
        P(),
    )
    return jax.shard_map(
        local,
        mesh=mesh,
        in_specs=placed,
        out_specs=(
            P(("region", "cluster"), None, None),
            P(("region", "cluster"), None, None),
            P(("region", "cluster")),
        ),
        check_vma=False,
    )
```

profile of v0, /device:TPU:0, one launch (start us, length us, event | category | flops | bytes accessed | tf_op | source)
XLA Modules:
  0.0 153.7 jit_solution(528623752502533669)
XLA Ops:
  7.2 0.0 copy-start.2
  7.2 0.0 all-reduce.3.cloned.1.call-start
  7.3 0.0 copy-start
  7.3 0.9 fusion.7
  8.2 0.9 broadcast_compare_fusion
  9.1 0.0 copy-start.4
  9.1 0.0 copy-start.5
  9.1 0.0 copy-start.6
  9.1 5.3 %multiply_reduce_fusion.1 = (f32[4]{0:T(128)S(1)}, f32[4,8,1024]{2,1,0:T(8,128)S(1)}) fusion(f32[4,8,1024]{2,1,0:T(8,128)} %param.14, f32[4]{0:T(128)} %param.15, f32[4,8,1024]{2,1,0:T(8,128)} %param.13, bf16[4,1024,1024]{2,1,0:T(8,128)(2,1)} %param.9, bf16[4,8,1024]{2,1,0:T(8,128)(2,1)} %param.10, pred[4,1024]{1,0:T(4,128)(4,1)S(1)} %broadcast_compare_fusion), kind=kOutput, calls=%fused_computation.10 | convolution fusion | flops 67305472 | bytes 8851488 | tf_op jit(solution)/shard_map/amr,arl->aml/dot_general | solution.py:34
  14.4 0.0 copy-start.1
  14.4 0.0 copy-done.2
  14.4 0.0 copy-done
  14.4 2.3 %multiply_reduce_fusion = (f32[4,1024]{1,0:T(4,128)S(1)}, f32[4,8,1024]{2,1,0:T(8,128)S(1)}) fusion(bf16[4,1024,1024]{2,1,0:T(8,128)(2,1)S(1)} %copy-done, f32[4,8,1024]{2,1,0:T(8,128)S(1)} %get-tuple-element.11, bf16[4,8,1024]{2,1,0:T(8,128)(2,1)S(1)} %copy-done.2, pred[4,1024]{1,0:T(4,128)(4,1)S(1)} %broadcast_compare_fusion), kind=kOutput, calls=%fused_computation.9 | convolution fusion | flops 67301376 | bytes 8736768 | tf_op jit(solution)/shard_map/aml,arl->amr/dot_general | solution.py:38
  16.7 0.0 copy-done.4
  16.7 0.1 select_bitcast_fusion
  16.8 21.9 %scatter_custom_fusion = f32[49152]{0:T(1024)S(1)} fusion(s32[4096]{0:T(1024)S(1)} %bitcast.17, f32[4096]{0:T(1024)S(1)} %bitcast.18, f32[]{:T(128)} %constant.68.clone.1), kind=kCustom, calls=%fused_computation.11 | custom fusion | flops 4096 | bytes 196612 | tf_op jit(solution)/shard_map/scatter-add | solution.py:50
  38.8 3.0 %collective-permute-start = (f32[16384]{0:T(1024)S(1)}, f32[16384]{0:T(1024)S(1)}, u32[]{:S(2)}, u32[]{:S(2)}) collective-permute-start(f32[16384]{0:T(1024)S(1)} %get-tuple-element.3), channel_id=1, source_target_pairs={{24,0},{0,8},{8,16},{16,24},{25,1},{1,9},{9,17},{17,25},{26,2},{2,... | collective-permute-start | bytes 196616 | tf_op jit(solution)/shard_map/ppermute | solution.py:14
  41.8 1.0 collective-permute-start.1
  42.8 0.7 dynamic_slice.3
  43.5 1.6 %collective-permute-done = f32[16384]{0:T(1024)S(1)} collective-permute-done((f32[16384]{0:T(1024)S(1)}, f32[16384]{0:T(1024)S(1)}, u32[]{:S(2)}, u32[]{:S(2)}) %collective-permute-start) | collective-permute-done | bytes 65568 | tf_op jit(solution)/shard_map/ppermute | solution.py:14
  45.1 1.4 collective-permute-done.1
  46.5 0.6 fusion.3
  47.1 0.0 all-reduce.3.cloned.1.call-update
  47.2 0.0 copy-done.5
  47.2 0.1 select_reduce_fusion
  47.3 0.0 copy-done.6
  47.3 0.6 dynamic-slice
  48.5 53.2 %all-reduce.3.cloned.1.call-done = f32[16384]{0:T(1024)} async-done(((f32[16384]{0:T(1024)}), f32[16384]{0:T(1024)}) %all-reduce.3.cloned.1.call-update) | async-done | bytes 65552
  101.7 0.7 fusion.11
  102.4 0.0 copy-start.3
  102.4 14.0 %all_gather.3 = f32[16384]{0:T(1024)S(1)} all-gather(f32[2048]{0:T(1024)S(1)} %fusion.11), channel_id=1, replica_groups=mesh['region'=4,'cluster'=8] {'cluster'}, dimensions={0}, use_global_device_ids=true | all-gather | bytes 73728 | tf_op jit(solution)/shard_map/all_gather | solution.py:56
  116.4 1.5 collective-permute-start.2
  117.8 1.5 collective-permute-start.3
  119.3 2.6 %collective-permute-done.2 = f32[16384]{0:T(1024)S(1)} collective-permute-done((f32[16384]{0:T(1024)S(1)}, f32[16384]{0:T(1024)S(1)}, u32[]{:S(2)}, u32[]{:S(2)}) %collective-permute-start.2) | collective-permute-done | bytes 65568 | tf_op jit(solution)/shard_map/ppermute | solution.py:14
  121.9 1.1 collective-permute-done.3
  123.0 23.0 %gather_fusion = f32[4096]{0:T(1024)S(1)} fusion(f32[49152]{0:T(1024)S(1)} %pad_maximum_fusion, s32[4096]{0:T(1024)S(1)} %bitcast_clamp_fusion), kind=kCustom, calls=%fused_computation | custom fusion | bytes 49152 | tf_op jit(solution)/shard_map/gather | solution.py:60
  146.1 0.0 copy-done.1
  146.1 0.0 copy-done.3
  146.1 0.7 select_convert_fusion
  (8 shorter events, 0.1 us)
Async XLA Ops:
  7.2 7.2 %copy-start.2 = (bf16[4,8,1024]{2,1,0:T(8,128)(2,1)S(1)}, bf16[4,8,1024]{2,1,0:T(8,128)(2,1)}, u32[]{:S(2)}) copy-start(bf16[4,8,1024]{2,1,0:T(8,128)(2,1)} %param.10) | copy-start | bytes 196612
  7.2 94.5 %all-reduce.3.cloned.1.call-start = ((), (), s32[]{:S(2)}) async-start(), calls=%async_computation | async-start | bytes 131072
  7.3 7.1 %copy-start = (bf16[4,1024,1024]{2,1,0:T(8,128)(2,1)S(1)}, bf16[4,1024,1024]{2,1,0:T(8,128)(2,1)}, u32[]{:S(2)}) copy-start(bf16[4,1024,1024]{2,1,0:T(8,128)(2,1)} %param.9) | copy-start | bytes 25165828
  9.1 7.7 %copy-start.4 = (s32[4]{0:T(128)S(1)}, s32[4]{0:T(128)}, u32[]{:S(2)}) copy-start(s32[4]{0:T(128)} %param.12) | copy-start | bytes 52
  9.1 38.1 %copy-start.5 = (f32[16]{0:T(128)S(1)}, f32[16]{0:T(128)}, u32[]{:S(2)}) copy-start(f32[16]{0:T(128)} %param.17) | copy-start | bytes 196
  9.1 38.2 %copy-start.6 = (u32[32]{0:T(128)S(1)}, u32[32]{0:T(128)}, u32[]{:S(2)}) copy-start(u32[32]{0:T(128)} %constant.94) | copy-start | bytes 388
  14.4 131.7 %copy-start.1 = (f32[4,8,1024]{2,1,0:T(8,128)}, f32[4,8,1024]{2,1,0:T(8,128)S(1)}, u32[]{:S(2)}) copy-start(f32[4,8,1024]{2,1,0:T(8,128)S(1)} %get-tuple-element.11) | copy-start | bytes 393220
  38.8 6.3 %collective-permute-start = (f32[16384]{0:T(1024)S(1)}, f32[16384]{0:T(1024)S(1)}, u32[]{:S(2)}, u32[]{:S(2)}) collective-permute-start(f32[16384]{0:T(1024)S(1)} %get-tuple-element.3), channel_id=1, source_target_pairs={{24,0},{0,8},{8,16},{16,24},{25,1},{1,9},{9,17},{17,25},{26,2},{2,... | collective-permute-start | bytes 196616 | tf_op jit(solution)/shard_map/ppermute | solution.py:14
  41.8 4.7 %collective-permute-start.1 = (f32[16384]{0:T(1024)S(1)}, f32[16384]{0:T(1024)S(1)}, u32[]{:S(2)}, u32[]{:S(2)}) collective-permute-start(f32[16384]{0:T(1024)S(1)} %get-tuple-element.4), channel_id=1, source_target_pairs={{8,0},{16,8},{24,16},{0,24},{9,1},{17,9},{25,17},{1,25},{10,2},{18... | collective-permute-start | bytes 196616 | tf_op jit(solution)/shard_map/ppermute | solution.py:14
  102.4 43.7 %copy-start.3 = (f32[2048]{0:T(1024)}, f32[2048]{0:T(1024)S(1)}, u32[]{:S(2)}) copy-start(f32[2048]{0:T(1024)S(1)} %fusion.11) | copy-start | bytes 24580
  116.4 5.5 %collective-permute-start.2 = (f32[16384]{0:T(1024)S(1)}, f32[16384]{0:T(1024)S(1)}, u32[]{:S(2)}, u32[]{:S(2)}) collective-permute-start(f32[16384]{0:T(1024)S(1)} %all_gather.3), channel_id=1, source_target_pairs={{24,0},{0,8},{8,16},{16,24},{25,1},{1,9},{9,17},{17,25},{26,2},{2,... | collective-permute-start | bytes 196616 | tf_op jit(solution)/shard_map/ppermute | solution.py:14
  117.8 5.2 %collective-permute-start.3 = (f32[16384]{0:T(1024)S(1)}, f32[16384]{0:T(1024)S(1)}, u32[]{:S(2)}, u32[]{:S(2)}) collective-permute-start(f32[16384]{0:T(1024)S(1)} %all_gather.3), channel_id=1, source_target_pairs={{8,0},{16,8},{24,16},{0,24},{9,1},{17,9},{25,17},{1,25},{10,2},{18... | collective-permute-start | bytes 196616 | tf_op jit(solution)/shard_map/ppermute | solution.py:14
Sparse Core Ops, SparseCore 0:
  47.3 54.3 all-reduce.2
where the time goes:
time: 154 us
  waiting for transfers between devices  59.9 us (39%)
  other arithmetic  26 us (17%)
  local copies, waits for them, and re-layouts  24.4 us (16%)
  between operations  14.9 us (10%)
  blocking collectives  14 us (9%)
  matrix products  7.59 us (5%)
  starting transfers between devices  6.97 us (5%)
    unnamed x2, waiting for transfers between devices  53.2 us
    gather x2, local copies, waits for them, and re-layouts, local(): rate = nearby[relative]  23 us
    scatter-add x1, other arithmetic, local(): jax.ops.segment_sum(flat_llr, relative.reshape(-1), num_segments=3 * regi...  21.9 us
    all_gather x1, blocking collectives, local(): own_post = lax.all_gather(owned, 'cluster', axis=0, tiled=True)  14 us
    ppermute x4, starting transfers between devices, passed_along(): return lax.ppermute(block, axis, route)  6.94 us
    ppermute x4, waiting for transfers between devices, passed_along(): return lax.ppermute(block, axis, route)  6.68 us
    dot_general x1, matrix products, local(): jnp.einsum('amr,arl->aml', masked, pilots, preferred_element_type=jnp.flo...  5.3 us
  transfers between devices with their start and end apart: 5, of which 5 were waited for; matrix products, arithmetic and copies ran while one was open for 1% of the time, Pallas kernels for 0%

commit v1 on v0

--- a/solution.py
+++ b/solution.py
@@ -53,7 +53,14 @@
     region_sum = window[region_users : 2 * region_users] + from_below + from_above
     owned_sum = lax.psum_scatter(region_sum, "cluster", scatter_dimension=0, tiled=True)
     owned = decide(owned_sum, own_start, U_DEV, user_cluster, cluster_prior)
-    own_post = lax.all_gather(owned, "cluster", axis=0, tiled=True)
+    ring = [owned]
+    for hop in range(7):
+        ring.append(lax.ppermute(ring[-1], "cluster", [(dev, (dev + 1) % 8) for dev in range(8)]))
+    own_post = jnp.roll(
+        jnp.concatenate(ring[::-1], axis=0),
+        (lax.axis_index("cluster") + 1) * ring[0].shape[0],
+        axis=0,
+    )
     below = passed_along(own_post, "region", 1)
     above = passed_along(own_post, "region", -1)
     nearby = jnp.concatenate([below, own_post, above])

time: 154 us -> 175 us (1.14)
  waiting for transfers between devices: 59.9 us -> 95.4 us
  blocking collectives: 14 us -> 0 us
    ppermute x0 -> x7, waiting for transfers between devices: none -> 34.1 us  [local(): lax.ppermute(ring[-1], 'cluster', [(dev, (dev + 1) % 8) for dev in range(...]
    all_gather x1 -> x0, blocking collectives: 14 us -> none  [local(): own_post = lax.all_gather(owned, 'cluster', axis=0, tiled=True)]
  transfers between devices with their start and end apart: 5 -> 12, of which waited for: 5 -> 12; matrix products, arithmetic and copies ran while one was open for 1% -> 1% of each run, Pallas kernels for 0% -> 0%
where the time goes in v1:
time: 175 us
  waiting for transfers between devices  95.4 us (55%)
  other arithmetic  26 us (15%)
  local copies, waits for them, and re-layouts  24.4 us (14%)
  between operations  15 us (9%)
  matrix products  7.59 us (4%)
  starting transfers between devices  6.56 us (4%)
    unnamed x2, waiting for transfers between devices  53.2 us
    ppermute x7, waiting for transfers between devices, local(): lax.ppermute(ring[-1], 'cluster', [(dev, (dev + 1) % 8) for dev in range(...  34.1 us
    gather x2, local copies, waits for them, and re-layouts, local(): rate = nearby[relative]  23 us
    scatter-add x1, other arithmetic, local(): jax.ops.segment_sum(flat_llr, relative.reshape(-1), num_segments=3 * regi...  21.9 us
    ppermute x4, waiting for transfers between devices, passed_along(): return lax.ppermute(block, axis, route)  8.14 us
    ppermute x4, starting transfers between devices, passed_along(): return lax.ppermute(block, axis, route)  6.44 us
    dot_general x1, matrix products, local(): jnp.einsum('amr,arl->aml', masked, pilots, preferred_element_type=jnp.flo...  5.3 us
  transfers between devices with their start and end apart: 12, of which 12 were waited for; matrix products, arithmetic and copies ran while one was open for 1% of the time, Pallas kernels for 0%

profile of v1, /device:TPU:0, one launch (start us, length us, event | category | flops | bytes accessed | tf_op | source)
XLA Modules:
  0.0 175.0 jit_solution(8452917627132282199)
XLA Ops:
  7.2 0.0 copy-start.2
  7.2 0.0 all-reduce.3.cloned.1.call-start
  7.3 0.0 copy-start
  7.3 0.9 fusion.7
  8.2 0.9 broadcast_compare_fusion
  9.1 0.0 copy-start.4
  9.1 0.0 copy-start.5
  9.1 0.0 copy-start.6
  9.1 5.3 %multiply_reduce_fusion.1 = (f32[4]{0:T(128)S(1)}, f32[4,8,1024]{2,1,0:T(8,128)S(1)}) fusion(f32[4,8,1024]{2,1,0:T(8,128)} %param.14, f32[4]{0:T(128)} %param.15, f32[4,8,1024]{2,1,0:T(8,128)} %param.13, bf16[4,1024,1024]{2,1,0:T(8,128)(2,1)} %param.9, bf16[4,8,1024]{2,1,0:T(8,128)(2,1)} %param.10, pred[4,1024]{1,0:T(4,128)(4,1)S(1)} %broadcast_compare_fusion), kind=kOutput, calls=%fused_computation.10 | convolution fusion | flops 67305472 | bytes 8851488 | tf_op jit(solution)/shard_map/amr,arl->aml/dot_general | solution.py:34
  14.4 0.0 copy-start.1
  14.4 0.0 copy-done.2
  14.4 0.0 copy-done
  14.4 2.3 %multiply_reduce_fusion = (f32[4,1024]{1,0:T(4,128)S(1)}, f32[4,8,1024]{2,1,0:T(8,128)S(1)}) fusion(bf16[4,1024,1024]{2,1,0:T(8,128)(2,1)S(1)} %copy-done, f32[4,8,1024]{2,1,0:T(8,128)S(1)} %get-tuple-element.11, bf16[4,8,1024]{2,1,0:T(8,128)(2,1)S(1)} %copy-done.2, pred[4,1024]{1,0:T(4,128)(4,1)S(1)} %broadcast_compare_fusion), kind=kOutput, calls=%fused_computation.9 | convolution fusion | flops 67301376 | bytes 8736768 | tf_op jit(solution)/shard_map/aml,arl->amr/dot_general | solution.py:38
  16.7 0.0 copy-done.4
  16.7 0.1 select_bitcast_fusion
  16.8 21.9 %scatter_custom_fusion = f32[49152]{0:T(1024)S(1)} fusion(s32[4096]{0:T(1024)S(1)} %bitcast.17, f32[4096]{0:T(1024)S(1)} %bitcast.18, f32[]{:T(128)} %constant.86.clone.1), kind=kCustom, calls=%fused_computation.11 | custom fusion | flops 4096 | bytes 196612 | tf_op jit(solution)/shard_map/scatter-add | solution.py:50
  38.8 3.0 %collective-permute-start = (f32[16384]{0:T(1024)S(1)}, f32[16384]{0:T(1024)S(1)}, u32[]{:S(2)}, u32[]{:S(2)}) collective-permute-start(f32[16384]{0:T(1024)S(1)} %get-tuple-element.3), channel_id=1, source_target_pairs={{24,0},{0,8},{8,16},{16,24},{25,1},{1,9},{9,17},{17,25},{26,2},{2,... | collective-permute-start | bytes 196616 | tf_op jit(solution)/shard_map/ppermute | solution.py:14
  41.8 1.0 collective-permute-start.1
  42.8 0.7 dynamic_slice.7
  43.5 1.6 collective-permute-done
  45.1 1.4 collective-permute-done.1
  46.5 0.6 fusion.3
  47.1 0.0 all-reduce.3.cloned.1.call-update
  47.2 0.0 copy-done.5
  47.2 0.1 select_reduce_fusion
  47.3 0.0 copy-done.6
  47.3 0.6 dynamic-slice
  48.5 53.2 %all-reduce.3.cloned.1.call-done = f32[16384]{0:T(1024)} async-done(((f32[16384]{0:T(1024)}), f32[16384]{0:T(1024)}) %all-reduce.3.cloned.1.call-update) | async-done | bytes 65552
  101.7 0.7 fusion.11
  102.4 0.0 copy-start.3
  102.4 0.1 collective-permute-start.2
  102.5 4.9 %collective-permute-done.2 = f32[2048]{0:T(1024)S(1)} collective-permute-done((f32[2048]{0:T(1024)S(1)}, f32[2048]{0:T(1024)S(1)}, u32[]{:S(2)}, u32[]{:S(2)}) %collective-permute-start.2) | collective-permute-done | bytes 8224 | tf_op jit(solution)/shard_map/ppermute | solution.py:58
  107.3 0.0 collective-permute-start.3
  107.3 4.9 %collective-permute-done.3 = f32[2048]{0:T(1024)S(1)} collective-permute-done((f32[2048]{0:T(1024)S(1)}, f32[2048]{0:T(1024)S(1)}, u32[]{:S(2)}, u32[]{:S(2)}) %collective-permute-start.3) | collective-permute-done | bytes 8224 | tf_op jit(solution)/shard_map/ppermute | solution.py:58
  112.2 0.0 collective-permute-start.4
  112.2 4.9 %collective-permute-done.4 = f32[2048]{0:T(1024)S(1)} collective-permute-done((f32[2048]{0:T(1024)S(1)}, f32[2048]{0:T(1024)S(1)}, u32[]{:S(2)}, u32[]{:S(2)}) %collective-permute-start.4) | collective-permute-done | bytes 8224 | tf_op jit(solution)/shard_map/ppermute | solution.py:58
  117.1 0.0 collective-permute-start.5
  117.1 4.9 %collective-permute-done.5 = f32[2048]{0:T(1024)S(1)} collective-permute-done((f32[2048]{0:T(1024)S(1)}, f32[2048]{0:T(1024)S(1)}, u32[]{:S(2)}, u32[]{:S(2)}) %collective-permute-start.5) | collective-permute-done | bytes 8224 | tf_op jit(solution)/shard_map/ppermute | solution.py:58
  121.9 0.0 collective-permute-start.6
  121.9 4.9 %collective-permute-done.6 = f32[2048]{0:T(1024)S(1)} collective-permute-done((f32[2048]{0:T(1024)S(1)}, f32[2048]{0:T(1024)S(1)}, u32[]{:S(2)}, u32[]{:S(2)}) %collective-permute-start.6) | collective-permute-done | bytes 8224 | tf_op jit(solution)/shard_map/ppermute | solution.py:58
  126.8 0.0 collective-permute-start.7
  126.8 4.9 %collective-permute-done.7 = f32[2048]{0:T(1024)S(1)} collective-permute-done((f32[2048]{0:T(1024)S(1)}, f32[2048]{0:T(1024)S(1)}, u32[]{:S(2)}, u32[]{:S(2)}) %collective-permute-start.7) | collective-permute-done | bytes 8224 | tf_op jit(solution)/shard_map/ppermute | solution.py:58
  131.7 0.0 collective-permute-start.8
  131.7 4.9 %collective-permute-done.8 = f32[2048]{0:T(1024)S(1)} collective-permute-done((f32[2048]{0:T(1024)S(1)}, f32[2048]{0:T(1024)S(1)}, u32[]{:S(2)}, u32[]{:S(2)}) %collective-permute-start.8) | collective-permute-done | bytes 8224 | tf_op jit(solution)/shard_map/ppermute | solution.py:58
  136.7 2.4 %collective-permute-start.10 = (f32[16384]{0:T(1024)S(1)}, f32[16384]{0:T(1024)S(1)}, u32[]{:S(2)}, u32[]{:S(2)}) collective-permute-start(f32[16384]{0:T(1024)S(1)} %dynamic_slice.8), channel_id=1, source_target_pairs={{8,0},{16,8},{24,16},{0,24},{9,1},{17,9},{25,17},{1,25},{10,2},{18... | collective-permute-start | bytes 196616 | tf_op jit(solution)/shard_map/ppermute | solution.py:14
  139.2 0.0 collective-permute-start.9
  139.2 1.9 %collective-permute-done.10 = f32[16384]{0:T(1024)S(1)} collective-permute-done((f32[16384]{0:T(1024)S(1)}, f32[16384]{0:T(1024)S(1)}, u32[]{:S(2)}, u32[]{:S(2)}) %collective-permute-start.10) | collective-permute-done | bytes 65568 | tf_op jit(solution)/shard_map/ppermute | solution.py:14
  141.1 3.3 %collective-permute-done.9 = f32[16384]{0:T(1024)S(1)} collective-permute-done((f32[16384]{0:T(1024)S(1)}, f32[16384]{0:T(1024)S(1)}, u32[]{:S(2)}, u32[]{:S(2)}) %collective-permute-start.9) | collective-permute-done | bytes 65568 | tf_op jit(solution)/shard_map/ppermute | solution.py:14
  144.3 23.0 %gather_fusion = f32[4096]{0:T(1024)S(1)} fusion(f32[49152]{0:T(1024)S(1)} %pad_maximum_fusion, s32[4096]{0:T(1024)S(1)} %bitcast_clamp_fusion), kind=kCustom, calls=%fused_computation | custom fusion | bytes 49152 | tf_op jit(solution)/shard_map/gather | solution.py:67
  167.4 0.0 copy-done.1
  167.4 0.0 copy-done.3
  167.4 0.7 select_convert_fusion
  (25 shorter events, 0.1 us)
Async XLA Ops:
  7.2 7.2 %copy-start.2 = (bf16[4,8,1024]{2,1,0:T(8,128)(2,1)S(1)}, bf16[4,8,1024]{2,1,0:T(8,128)(2,1)}, u32[]{:S(2)}) copy-start(bf16[4,8,1024]{2,1,0:T(8,128)(2,1)} %param.10) | copy-start | bytes 196612
  7.2 94.5 %all-reduce.3.cloned.1.call-start = ((), (), s32[]{:S(2)}) async-start(), calls=%async_computation | async-start | bytes 131072
  7.3 7.1 %copy-start = (bf16[4,1024,1024]{2,1,0:T(8,128)(2,1)S(1)}, bf16[4,1024,1024]{2,1,0:T(8,128)(2,1)}, u32[]{:S(2)}) copy-start(bf16[4,1024,1024]{2,1,0:T(8,128)(2,1)} %param.9) | copy-start | bytes 25165828
  9.1 7.7 %copy-start.4 = (s32[4]{0:T(128)S(1)}, s32[4]{0:T(128)}, u32[]{:S(2)}) copy-start(s32[4]{0:T(128)} %param.12) | copy-start | bytes 52
  9.1 38.1 %copy-start.5 = (f32[16]{0:T(128)S(1)}, f32[16]{0:T(128)}, u32[]{:S(2)}) copy-start(f32[16]{0:T(128)} %param.17) | copy-start | bytes 196
  9.1 38.2 %copy-start.6 = (u32[32]{0:T(128)S(1)}, u32[32]{0:T(128)}, u32[]{:S(2)}) copy-start(u32[32]{0:T(128)} %constant.113) | copy-start | bytes 388
  14.4 153.0 %copy-start.1 = (f32[4,8,1024]{2,1,0:T(8,128)}, f32[4,8,1024]{2,1,0:T(8,128)S(1)}, u32[]{:S(2)}) copy-start(f32[4,8,1024]{2,1,0:T(8,128)S(1)} %get-tuple-element.11) | copy-start | bytes 393220
  38.8 6.3 %collective-permute-start = (f32[16384]{0:T(1024)S(1)}, f32[16384]{0:T(1024)S(1)}, u32[]{:S(2)}, u32[]{:S(2)}) collective-permute-start(f32[16384]{0:T(1024)S(1)} %get-tuple-element.3), channel_id=1, source_target_pairs={{24,0},{0,8},{8,16},{16,24},{25,1},{1,9},{9,17},{17,25},{26,2},{2,... | collective-permute-start | bytes 196616 | tf_op jit(solution)/shard_map/ppermute | solution.py:14
  41.8 4.7 %collective-permute-start.1 = (f32[16384]{0:T(1024)S(1)}, f32[16384]{0:T(1024)S(1)}, u32[]{:S(2)}, u32[]{:S(2)}) collective-permute-start(f32[16384]{0:T(1024)S(1)} %get-tuple-element.4), channel_id=1, source_target_pairs={{8,0},{16,8},{24,16},{0,24},{9,1},{17,9},{25,17},{1,25},{10,2},{18... | collective-permute-start | bytes 196616 | tf_op jit(solution)/shard_map/ppermute | solution.py:14
  102.4 65.0 %copy-start.3 = (f32[2048]{0:T(1024)}, f32[2048]{0:T(1024)S(1)}, u32[]{:S(2)}) copy-start(f32[2048]{0:T(1024)S(1)} %fusion.11) | copy-start | bytes 24580
  102.4 4.9 %collective-permute-start.2 = (f32[2048]{0:T(1024)S(1)}, f32[2048]{0:T(1024)S(1)}, u32[]{:S(2)}, u32[]{:S(2)}) collective-permute-start(f32[2048]{0:T(1024)S(1)} %fusion.11), channel_id=1, source_target_pairs={{0,1},{1,2},{2,3},{3,4},{4,5},{5,6},{6,7},{7,0},{8,9},{9,10},{10,1... | collective-permute-start | bytes 24584 | tf_op jit(solution)/shard_map/ppermute | solution.py:58
  107.3 4.9 %collective-permute-start.3 = (f32[2048]{0:T(1024)S(1)}, f32[2048]{0:T(1024)S(1)}, u32[]{:S(2)}, u32[]{:S(2)}) collective-permute-start(f32[2048]{0:T(1024)S(1)} %collective-permute-done.2), channel_id=1, source_target_pairs={{0,1},{1,2},{2,3},{3,4},{4,5},{5,6},{6,7},{7,0},{8,9},{9,10},{10,1... | collective-permute-start | bytes 24584 | tf_op jit(solution)/shard_map/ppermute | solution.py:58
  112.2 4.9 %collective-permute-start.4 = (f32[2048]{0:T(1024)S(1)}, f32[2048]{0:T(1024)S(1)}, u32[]{:S(2)}, u32[]{:S(2)}) collective-permute-start(f32[2048]{0:T(1024)S(1)} %collective-permute-done.3), channel_id=1, source_target_pairs={{0,1},{1,2},{2,3},{3,4},{4,5},{5,6},{6,7},{7,0},{8,9},{9,10},{10,1... | collective-permute-start | bytes 24584 | tf_op jit(solution)/shard_map/ppermute | solution.py:58
  117.1 4.9 %collective-permute-start.5 = (f32[2048]{0:T(1024)S(1)}, f32[2048]{0:T(1024)S(1)}, u32[]{:S(2)}, u32[]{:S(2)}) collective-permute-start(f32[2048]{0:T(1024)S(1)} %collective-permute-done.4), channel_id=1, source_target_pairs={{0,1},{1,2},{2,3},{3,4},{4,5},{5,6},{6,7},{7,0},{8,9},{9,10},{10,1... | collective-permute-start | bytes 24584 | tf_op jit(solution)/shard_map/ppermute | solution.py:58
  121.9 4.9 %collective-permute-start.6 = (f32[2048]{0:T(1024)S(1)}, f32[2048]{0:T(1024)S(1)}, u32[]{:S(2)}, u32[]{:S(2)}) collective-permute-start(f32[2048]{0:T(1024)S(1)} %collective-permute-done.5), channel_id=1, source_target_pairs={{0,1},{1,2},{2,3},{3,4},{4,5},{5,6},{6,7},{7,0},{8,9},{9,10},{10,1... | collective-permute-start | bytes 24584 | tf_op jit(solution)/shard_map/ppermute | solution.py:58
  126.8 4.9 %collective-permute-start.7 = (f32[2048]{0:T(1024)S(1)}, f32[2048]{0:T(1024)S(1)}, u32[]{:S(2)}, u32[]{:S(2)}) collective-permute-start(f32[2048]{0:T(1024)S(1)} %collective-permute-done.6), channel_id=1, source_target_pairs={{0,1},{1,2},{2,3},{3,4},{4,5},{5,6},{6,7},{7,0},{8,9},{9,10},{10,1... | collective-permute-start | bytes 24584 | tf_op jit(solution)/shard_map/ppermute | solution.py:58
  131.7 4.9 %collective-permute-start.8 = (f32[2048]{0:T(1024)S(1)}, f32[2048]{0:T(1024)S(1)}, u32[]{:S(2)}, u32[]{:S(2)}) collective-permute-start(f32[2048]{0:T(1024)S(1)} %collective-permute-done.7), channel_id=1, source_target_pairs={{0,1},{1,2},{2,3},{3,4},{4,5},{5,6},{6,7},{7,0},{8,9},{9,10},{10,1... | collective-permute-start | bytes 24584 | tf_op jit(solution)/shard_map/ppermute | solution.py:58
  136.7 4.3 %collective-permute-start.10 = (f32[16384]{0:T(1024)S(1)}, f32[16384]{0:T(1024)S(1)}, u32[]{:S(2)}, u32[]{:S(2)}) collective-permute-start(f32[16384]{0:T(1024)S(1)} %dynamic_slice.8), channel_id=1, source_target_pairs={{8,0},{16,8},{24,16},{0,24},{9,1},{17,9},{25,17},{1,25},{10,2},{18... | collective-permute-start | bytes 196616 | tf_op jit(solution)/shard_map/ppermute | solution.py:14
  139.2 5.2 %collective-permute-start.9 = (f32[16384]{0:T(1024)S(1)}, f32[16384]{0:T(1024)S(1)}, u32[]{:S(2)}, u32[]{:S(2)}) collective-permute-start(f32[16384]{0:T(1024)S(1)} %dynamic_slice.8), channel_id=1, source_target_pairs={{24,0},{0,8},{8,16},{16,24},{25,1},{1,9},{9,17},{17,25},{26,2},{2,... | collective-permute-start | bytes 196616 | tf_op jit(solution)/shard_map/ppermute | solution.py:14
Sparse Core Ops, SparseCore 0:
  47.3 54.3 all-reduce.2
